TPU v7x, 128 devices: a whole 4x4x4 slice. The times are simulated.
128 devices in a mesh: replica: 4 (over y_hi, core), fsdp: 32 (over y_lo, z, x).
Axes of the slice: x: 4, y: 4 (y_hi: 2, y_lo: 2; y = y_hi * 2 + y_lo), z: 4, core: 2. Of those that a mesh axis runs over, the one named last changes fastest.
Arguments:
- layer_input: bfloat16 [4, 16384, 4096], P('replica', 'fsdp'), may hold values from -36 to 36, as said below
- norm_gain: bfloat16 [4, 4096], P('replica', 'fsdp'), may hold values from 0.099609375 to 1.8984375
- kv_weight: bfloat16 [4, 4096, 1024], P('replica', 'fsdp'), may hold values from -0.09375 to 0.09375
- kv_cotangent: bfloat16 [4, 16384, 1024], P('replica', 'fsdp'), may hold values from -6 to 6
- pseudo_grad: float32 [4, 12288, 1024], P('replica', 'fsdp'), may hold values from -6 to 6
- outer_momentum: float32 [12288, 1024], P('fsdp'), may hold values from -6 to 6
- global_params: float32 [12288, 1024], P('fsdp'), may hold values from -6 to 6
- local_params: bfloat16 [4, 12288, 1024], P('replica', 'fsdp'), may hold values from -6 to 6
Outputs:
- kv_out: bfloat16 [4, 16384, 1024], P('replica', 'fsdp')
- input_grad: bfloat16 [4, 16384, 4096], P('replica', 'fsdp')
- kv_weight_grad: float32 [4, 4096, 1024], P('replica', 'fsdp')
- gain_grad: float32 [4, 4096], P('replica', 'fsdp')
- momentum_new: float32 [12288, 1024], P('fsdp')
- global_new: float32 [12288, 1024], P('fsdp')
- local_new: bfloat16 [4, 12288, 1024], P('replica', 'fsdp')
Inputs may be any that keep to these rules, and one draw needn't show every extreme that they name: `layer_input`: activations of the residual stream.
All inputs are finite; a program needn't handle non-finite values.
Results may differ from a plain program's by a relative error of at most 0.0049.
Values may be sent and summed in bfloat16 or wider, within the bound.
A program may use at most 128 MiB of HBM per device.

v0:
```python
import math

import jax
import jax.numpy as jnp
from jax import lax
from jax.sharding import PartitionSpec as P

HEAD = 128
SEQ_LEN = 4096


epsilon = 1e-05
rope_base = 500000.0
momentum_rate = 0.9
outer_rate = 0.7
mixing_rate = 0.5


def angles_for(positions, head):
    half = head // 2
    index_f = jnp.arange(half, dtype=jnp.float32)
    inverse = jnp.exp(index_f * (-2.0 * math.log(rope_base) / head))
    angle = positions.astype(jnp.float32)[:, None] * inverse[None, :]
    return (jnp.cos(angle), jnp.sin(angle))


def rotate_keys(keys, cosine, sine, head, sign):
    count = keys.shape[0]
    shaped = keys.reshape(count, -1, head)
    half = head // 2
    first = shaped[:, :, :half]
    second = shaped[:, :, half:]
    cos_b = cosine[:, None, :]
    sin_b = sine[:, None, :] * sign
    out = jnp.concatenate([first * cos_b - second * sin_b, second * cos_b + first * sin_b], axis=2)
    return out.reshape(count, -1)


def forward_piece(normed, weight_piece, gain_piece):
    gain_vals = gain_piece.astype(jnp.float32)
    hidden_piece = (normed * gain_vals[None, :]).astype(jnp.bfloat16)
    key_pre = jnp.dot(hidden_piece, weight_piece, preferred_element_type=jnp.float32)
    return (key_pre, hidden_piece, gain_vals)


def backward_piece(kv_grad, weight_piece):
    product = lax.dot_general(
        kv_grad, weight_piece, (((1,), (1,)), ((), ())), preferred_element_type=jnp.float32
    )
    return product


def local(
    layer_input,
    norm_gain,
    kv_weight,
    kv_cotangent,
    pseudo_grad,
    outer_momentum,
    global_params,
    local_params,
):
    tokens_in = layer_input[0]
    gain_shard = norm_gain[0]
    weight_shard = kv_weight[0]
    cotangent = kv_cotangent[0]
    rows, width = tokens_in.shape
    kvw = weight_shard.shape[1] // 2
    groups = lax.axis_size("fsdp")
    positions = (lax.axis_index("fsdp") * rows + jnp.arange(rows, dtype=jnp.int32)) % SEQ_LEN
    cosine, sine = angles_for(positions, HEAD)
    values = tokens_in.astype(jnp.float32)
    inv_rms = lax.rsqrt(jnp.mean(values * values, axis=-1, keepdims=True) + epsilon)
    normed = values * inv_rms
    key_back = rotate_keys(cotangent[:, :kvw].astype(jnp.float32), cosine, sine, HEAD, -1.0).astype(
        jnp.bfloat16
    )
    kv_grad = jnp.concatenate([key_back, cotangent[:, kvw:]], axis=1)
    key_pre, hidden, gain_full = forward_piece(
        normed,
        lax.all_gather(weight_shard, "fsdp", axis=0, tiled=True),
        lax.all_gather(gain_shard, "fsdp", axis=0, tiled=True),
    )
    hidden_grad = backward_piece(kv_grad, lax.all_gather(weight_shard, "fsdp", axis=0, tiled=True))
    kv_out = jnp.concatenate(
        [rotate_keys(key_pre[:, :kvw], cosine, sine, HEAD, 1.0), key_pre[:, kvw:]], axis=1
    ).astype(jnp.bfloat16)
    scale = 1.0 / math.sqrt(rows * groups)
    gain_product = hidden_grad * normed
    weight_term = (
        lax.dot_general(
            hidden, kv_grad, (((0,), (0,)), ((), ())), preferred_element_type=jnp.float32
        )
        * scale
    )
    gain_term = jnp.sum(gain_product, axis=0) * scale
    weight_grad, gain_grad = (
        lax.psum_scatter(weight_term, "fsdp", scatter_dimension=0, tiled=True),
        lax.psum_scatter(gain_term, "fsdp", scatter_dimension=0, tiled=True),
    )
    normed_grad = hidden_grad * gain_full
    input_grad = (
        inv_rms * (normed_grad - normed * jnp.mean(normed_grad * normed, axis=-1, keepdims=True))
    ).astype(jnp.bfloat16)
    pseudo = pseudo_grad[0]
    replicas = lax.axis_size("replica")
    total = lax.psum(pseudo, "replica")
    average = total / replicas
    momentum_new = momentum_rate * outer_momentum + average
    global_new = global_params - outer_rate * (average + momentum_rate * momentum_new)
    local_new = (
        mixing_rate * local_params[0].astype(jnp.float32) + (1.0 - mixing_rate) * global_new
    ).astype(jnp.bfloat16)
    return (
        kv_out[None],
        input_grad[None],
        weight_grad[None],
        gain_grad[None],
        momentum_new,
        global_new,
        local_new[None],
    )


def solution(mesh):
    in_specs = (
        P("replica", "fsdp", None),
        P("replica", "fsdp"),
        P("replica", "fsdp", None),
        P("replica", "fsdp", None),
        P("replica", "fsdp", None),
        P("fsdp", None),
        P("fsdp", None),
        P("replica", "fsdp", None),
    )
    out_specs = (
        P("replica", "fsdp", None),
        P("replica", "fsdp", None),
        P("replica", "fsdp", None),
        P("replica", "fsdp"),
        P("fsdp", None),
        P("fsdp", None),
        P("replica", "fsdp", None),
    )
    return jax.shard_map(local, mesh=mesh, in_specs=in_specs, out_specs=out_specs, check_vma=False)
```

profile of v0, /device:TPU:0, one launch (start us, length us, event | category | flops | bytes accessed | tf_op | source)
XLA Modules:
  0.0 415.8 jit_solution(27503207839580185)
XLA Ops:
  8.0 0.0 copy-start.3
  8.0 0.0 all-gather.4.cloned.1.call-start
  8.1 0.7 all-gather.4.cloned.1.call-update
  8.7 0.0 all-reduce.3.cloned.1.call-start
  8.8 0.5 all-reduce.3.cloned.1.call-update
  9.3 0.0 reduce-scatter.2.cloned.1.call-start
  9.4 82.9 %all-gather = bf16[1,4096]{1,0:T(2,128)(2,1)S(1)} all-gather(bf16[1,128]{1,0:T(2,128)(2,1)} %param.9), channel_id=2, replica_groups=mesh['replica'=4,'fsdp'=32] {'fsdp'}, dimensions={1}, use_global_device_ids=true | all-gather | bytes 8448 | tf_op jit(solution)/shard_map/all_gather | solution.py:82
  92.3 3.1 fusion.10
  95.4 0.0 copy-done.3
  95.5 0.9 slice_convert_fusion.1
  96.4 0.4 reshape.172
  96.8 1.8 broadcast_multiply_fusion.1
  98.6 80.9 %all-gather.4.cloned.1.call-done = bf16[1,4096,1024]{2,1,0:T(8,128)(2,1)} async-done(((bf16[1,128,1024]{2,1,0:T(8,128)(2,1)}), bf16[1,4096,1024]{2,1,0:T(8,128)(2,1)}) %all-gather.4.cloned.1.call-update) | async-done | bytes 8388624 | tf_op jit(solution)/shard_map/all_gather | solution.py:81
  179.5 8.2 %fusion.13 = f32[512,1024]{1,0:T(8,128)S(1)} fusion(bf16[1,4096,1024]{2,1,0:T(8,128)(2,1)} %all-gather.4.cloned.1.call-done, bf16[1,512,4096]{2,1,0:T(8,128)(2,1)} %param.8, f32[4096]{0:T(1024)S(1)} %bitcast.41, f32[512]{0:T(512)S(1)} %add_rsqrt_fusion), kind=kOutput, calls=%fused_computation.15 | convolution fusion | flops 4303355904 | bytes 14698496 | tf_op jit(solution)/shard_map/dot_general | solution.py:42
  187.7 0.0 copy-start.2
  187.7 1.3 copy-done.2
  189.1 0.1 slice.33
  189.1 0.4 reshape.167
  189.5 0.0 copy-start
  189.5 0.0 copy-start.5
  189.5 2.7 subtract_convert_fusion
  192.3 1.4 pad_maximum_fusion.4
  193.7 0.1 copy.17
  193.8 0.0 copy-start.7
  193.8 0.0 copy-done
  193.8 0.0 copy-done.5
  193.8 8.3 %broadcast_multiply_fusion = f32[4096,1024]{1,0:T(8,128)} fusion(bf16[1,512,4096]{2,1,0:T(8,128)(2,1)S(1)} %copy-done, f32[4096]{0:T(1024)S(1)} %bitcast.42, f32[512]{0:T(512)S(1)} %add_rsqrt_fusion, bf16[512,512]{1,0:T(8,128)(2,1)S(1)} %copy-done.5, bf16[512,512]{1,0:T(8,128)(2,1)S(1)} %bitcast.39), kind=kOutput, calls=%fused_computation.17 | convolution fusion | flops 4309647360 | bytes 22038528 | tf_op jit(solution)/shard_map/dot_general | solution.py:91
  202.1 0.0 copy-done.7
  202.1 0.0 copy-start.8
  202.1 0.0 copy-start.1
  202.1 0.0 copy-start.4
  202.1 0.0 reduce-scatter.2.cloned.1.call-update
  202.1 0.6 copy-done.8
  202.8 0.6 dynamic-slice
  204.0 0.0 copy-start.6
  204.0 0.0 all-reduce.3.cloned.1.call-done
  204.0 0.0 copy-done.1
  204.1 0.0 copy-done.4
  204.1 4.6 %fusion.20 = (bf16[1,384,1024]{2,1,0:T(8,128)(2,1)}, f32[384,1024]{1,0:T(8,128)}, f32[384,1024]{1,0:T(8,128)}) fusion(bf16[1,384,1024]{2,1,0:T(8,128)(2,1)S(1)} %copy-done.4, f32[384,1024]{1,0:T(8,128)S(1)} %copy-done.1, f32[384,1024]{1,0:T(8,128)} %all-reduce.3.cloned.1.call-done, f32[384,1024]{1,0:T(8,128)} %param.13), kind=kLoop, calls=%fused_computation.31 | loop fusion | flops 4325376 | bytes 9437184 | tf_op jit(solution)/shard_map/broadcast_in_dim | solution.py:121
  208.7 0.2 concatenate.27
  208.9 0.0 copy-done.6
  208.9 13.6 %fusion.9 = (f32[4096]{0:T(1024)S(1)}, f32[512]{0:T(512)S(1)}, f32[512,4096]{1,0:T(8,128)}) fusion(bf16[1,512,4096]{2,1,0:T(8,128)(2,1)} %param.8, f32[512]{0:T(512)S(1)} %add_rsqrt_fusion, f32[4096]{0:T(1024)S(1)} %bitcast.43, bf16[1,4096,1024]{2,1,0:T(8,128)(2,1)} %all-gather.4.cloned.1.call-done, bf16[512,512]{1,0:T(8,128)(2,1)S(1)} %copy-done.6, ...), kind=kOutput, calls=%fused_computation.11 | convolution fusion | flops 4311739904 | bytes 22056960 | tf_op jit(solution)/shard_map/dot_general | solution.py:47
  222.4 158.3 %all-reduce = f32[4096]{0:T(1024)S(1)} all-reduce(f32[4096]{0:T(1024)S(1)} %broadcast_multiply_fusion.2), channel_id=5, replica_groups=mesh['replica'=4,'fsdp'=32] {'fsdp'}, use_global_device_ids=true, to_apply=%region_4.5.clone | all-reduce | flops 4096 | bytes 32768
  380.8 0.6 dynamic-slice_bitcast_fusion
  381.3 1.3 fusion.21
  382.6 1.1 pad_maximum_fusion
  383.8 7.3 %fusion.15 = bf16[1,512,4096]{2,1,0:T(8,128)(2,1)} fusion(f32[512,4096]{1,0:T(8,128)} %get-tuple-element.23, bf16[1,512,4096]{2,1,0:T(8,128)(2,1)} %param.8, f32[512]{0:T(512)S(1)} %broadcast_multiply_fusion.3, f32[4096]{0:T(1024)S(1)} %bitcast.44, f32[512]{0:T(512)S(1)} %add_rsqrt_fusion), kind=kLoop, calls=%fused_computation.18 | loop fusion | flops 14680064 | bytes 16797696 | tf_op jit(solution)/shard_map/broadcast_in_dim | solution.py:116
  391.1 17.3 %reduce-scatter.2.cloned.1.call-done = f32[128,1024]{1,0:T(8,128)} async-done(((f32[4096,1024]{1,0:T(8,128)}), f32[128,1024]{1,0:T(8,128)}) %reduce-scatter.2.cloned.1.call-update) | async-done | bytes 524304 | tf_op jit(solution)/shard_map/reduce_scatter | solution.py:98
  (6 shorter events, 0.1 us)
Async XLA Ops:
  8.0 87.4 %copy-start.3 = (bf16[1,512,1024]{2,1,0:T(8,128)(2,1)S(1)}, bf16[1,512,1024]{2,1,0:T(8,128)(2,1)}, u32[]{:S(2)}) copy-start(bf16[1,512,1024]{2,1,0:T(8,128)(2,1)} %param.11) | copy-start | bytes 3145732
  8.0 171.5 %all-gather.4.cloned.1.call-start = ((), (), s32[]{:S(2)}) async-start(), calls=%async_computation.3 | async-start | bytes 8650752 | tf_op jit(solution)/shard_map/all_gather | solution.py:81
  8.7 195.3 %all-reduce.3.cloned.1.call-start = ((), (), s32[]{:S(2)}) async-start(), calls=%async_computation.2 | async-start | bytes 3145728 | tf_op jit(solution)/shard_map/psum | solution.py:107
  9.3 399.1 %reduce-scatter.2.cloned.1.call-start = ((), (), s32[]{:S(2)}) async-start(), calls=%async_computation.1 | async-start | bytes 17301504 | tf_op jit(solution)/shard_map/reduce_scatter | solution.py:98
  187.7 1.3 copy-start.2
  189.5 4.3 %copy-start = (bf16[1,512,4096]{2,1,0:T(8,128)(2,1)S(1)}, bf16[1,512,4096]{2,1,0:T(8,128)(2,1)}, u32[]{:S(2)}) copy-start(bf16[1,512,4096]{2,1,0:T(8,128)(2,1)} %param.8) | copy-start | bytes 12582916
  189.5 4.3 %copy-start.5 = (bf16[512,512]{1,0:T(8,128)(2,1)S(1)}, bf16[512,512]{1,0:T(8,128)(2,1)}, u32[]{:S(2)}) copy-start(bf16[512,512]{1,0:T(8,128)(2,1)} %get-tuple-element.17) | copy-start | bytes 1572868
  193.8 8.3 %copy-start.7 = (bf16[64,8,4,128]{3,1,2,0:T(8,128)(2,1)}, bf16[64,8,4,128]{3,1,2,0:T(8,128)(2,1)S(1)}, u32[]{:S(2)}) copy-start(bf16[64,8,4,128]{3,1,2,0:T(8,128)(2,1)S(1)} %copy.17) | copy-start | bytes 1572868
  202.1 0.7 copy-start.8
  202.1 1.9 copy-start.1
  202.1 1.9 copy-start.4
  204.0 4.9 %copy-start.6 = (bf16[512,512]{1,0:T(8,128)(2,1)S(1)}, bf16[512,512]{1,0:T(8,128)(2,1)}, u32[]{:S(2)}) copy-start(bf16[512,512]{1,0:T(8,128)(2,1)} %get-tuple-element.17) | copy-start | bytes 1572868
Sparse Core Ops, SparseCore 0:
  10.5 168.9 all-gather.3
  202.3 206.0 reduce-scatter.1
Sparse Core Ops, SparseCore 1:
  11.7 70.8 all-reduce.2
where the time goes:
time: 416 us
  blocking collectives  241 us (58%)
  waiting for transfers between devices  99.4 us (24%)
  matrix products  30.1 us (7%)
  other arithmetic  23.1 us (6%)
  between operations  16.3 us (4%)
  local copies, waits for them, and re-layouts  5.51 us (1%)
    unnamed x1, blocking collectives  158 us
    all_gather x1, blocking collectives, local(): lax.all_gather(gain_shard, 'fsdp', axis=0, tiled=True)  82.9 us
    all_gather x1, waiting for transfers between devices, local(): lax.all_gather(weight_shard, 'fsdp', axis=0, tiled=True)  80.9 us
    reduce_scatter x1, waiting for transfers between devices, local(): lax.psum_scatter(weight_term, 'fsdp', scatter_dimension=0, tiled=True)  17.3 us
    dot_general x1, matrix products, backward_piece(): lax.dot_general(kv_grad, weight_piece, (((1,), (1,)), ((), ())), preferre...  13.6 us
  transfers between devices with their start and end apart: 3, of which 2 were waited for; matrix products, arithmetic and copies ran while one was open for 14% of the time, Pallas kernels for 0%

commit v1 on v0

v1 whole, which is shorter than its diff:
```python
import math

import jax
import jax.numpy as jnp
from jax import lax
from jax.experimental import pallas as pl
from jax.experimental.pallas import tpu as pltpu
from jax.sharding import PartitionSpec as P

HEAD = 128
SEQ_LEN = 4096
D = 4096
KV = 1024
TOK = 512
ROWS = 128
PARTS = 2
PSR = 384

epsilon = 1e-05
rope_base = 500000.0
momentum_rate = 0.9
outer_rate = 0.7
mixing_rate = 0.5

MESH = pl.DeviceIdType.MESH
BF = jnp.bfloat16
F32 = jnp.float32

SCATTER_ORDER = ((1, 2), (1, 1), (1, 3), (1, 0), (0, 2), (0, 1), (0, 3), (0, 0))
PER_PART = 41


def key_y(p):
    return p * PER_PART


def key_1(p, yr, step, way):
    return p * PER_PART + 1 + yr * 4 + step * 2 + way


def key_2(p, g, step, way):
    return p * PER_PART + 9 + (g[0] * 4 + g[1]) * 4 + step * 2 + way


def kernel(
    x_hbm,
    gain_hbm,
    w_hbm,
    ct_hbm,
    ps_hbm,
    om_hbm,
    gp_hbm,
    lp_hbm,
    cos_hbm,
    sin_hbm,
    kv_out,
    ig_out,
    wg_out,
    gg_out,
    mom_out,
    glob_out,
    loc_out,
    x_v,
    hid,
    wbuf,
    kv,
    kvt,
    pt,
    x1,
    x2,
    ybuf,
    gbuf,
    grow,
    invb,
    cb,
    pre,
    cos_v,
    sin_v,
    ps,
    psr,
    psum,
    srecv,
    trecv,
    om,
    gp,
    lp,
    lsem,
    ag_s,
    ag_r,
    rs_s,
    rs_r,
    g_s,
    g_r,
    p_s,
    p_r,
):
    rep = lax.axis_index("replica")
    me = lax.axis_index("fsdp")
    y = me // 16
    zc = (me // 4) % 4
    xc = me % 4
    core = rep % 2

    def at(yr, zo, xo):
        yy = y if yr == 0 else 1 - y
        zz = zc if zo == 0 else (zc + zo) % 4
        xx = xc if xo == 0 else (xc + xo) % 4
        return yy * 16 + zz * 4 + xx

    def shard(p, yr, o1, o2):
        return at(yr, o1, o2) if p == 0 else at(yr, o2, o1)

    shards = {
        (p, yr, o1, o2): shard(p, yr, o1, o2)
        for p in range(PARTS)
        for yr in range(2)
        for o1 in range(4)
        for o2 in range(4)
    }
    ypeer = at(1, 0, 0)
    peers1 = {(p, way): shards[p, 0, 1 if way == 0 else 3, 0] for p in range(PARTS) for way in range(2)}
    peers2 = {(p, way): shards[p, 0, 0, 1 if way == 0 else 3] for p in range(PARTS) for way in range(2)}
    gpeers = [at(0, 0, 1), at(0, 0, 2), at(0, 0, 3), at(0, 1, 0), at(0, 2, 0), at(0, 3, 0), ypeer]
    twin = rep + 1 - 2 * core
    across = (rep + 2) % 4
    half = 192
    mine = pl.multiple_of(core * half, half)
    other = pl.multiple_of((1 - core) * half, half)

    loads = {}

    def load(name, src, dst, k):
        loads[name] = pltpu.make_async_copy(src, dst, lsem.at[k])
        loads[name].start()

    own_rows = pl.multiple_of(me * ROWS, ROWS)
    load("w", w_hbm, wbuf.at[pl.ds(own_rows, ROWS)], 0)
    load("gain", gain_hbm, gbuf.at[me], 1)
    load("ps", ps_hbm, ps, 2)
    load("ct", ct_hbm, kv, 3)
    load("cos", cos_hbm, cos_v, 4)
    load("sin", sin_hbm, sin_v, 5)
    load("x", x_hbm, x_v, 6)
    load("om", om_hbm, om, 7)
    load("gp", gp_hbm, gp, 8)
    load("lp", lp_hbm, lp, 9)

    barrier = pltpu.get_barrier_semaphore()
    greet = [(rep, d) for d in gpeers] + [(twin, me), (across, me)]
    for dev in greet:
        pl.semaphore_signal(barrier, inc=1, device_id=dev, device_id_type=MESH)
    pl.semaphore_wait(barrier, len(greet))

    sent = []

    def remote(src, dst, ss, rs, dev):
        return pltpu.make_async_remote_copy(
            src_ref=src, dst_ref=dst, send_sem=ss, recv_sem=rs, device_id=dev, device_id_type=MESH
        )

    def wrows(p, s, piece):
        if piece is None:
            return wbuf.at[pl.ds(pl.multiple_of(s * ROWS + p * 64, 64), 64)]
        return wbuf.at[pl.ds(pl.multiple_of(s * ROWS + p * 64 + piece * 32, 32), 32)]

    def ag_send(p, s, piece, k, dev):
        ref = wrows(p, s, piece)
        remote(ref, ref, ag_s.at[k], ag_r.at[k], (rep, dev)).start()

    def ag_wait(p, s, piece, k):
        ref = wrows(p, s, piece)
        remote(ref, ref, ag_s.at[k], ag_r.at[k], (rep, ypeer)).wait_recv()

    def ag_y_send():
        for p in range(PARTS):
            ag_send(p, me, None, key_y(p), ypeer)

    def ag_y_wait():
        for p in range(PARTS):
            ag_wait(p, ypeer, None, key_y(p))

    def ag1_first(yr):
        for p in range(PARTS):
            for way in range(2):
                ag_send(p, shards[p, yr, 0, 0], None, key_1(p, yr, 0, way), peers1[p, way])

    def ag1_next(yr):
        for p in range(PARTS):
            for way in range(2):
                s = shards[p, yr, 3 if way == 0 else 1, 0]
                ag_wait(p, s, None, key_1(p, yr, 0, way))
                ag_send(p, s, way, key_1(p, yr, 1, way), peers1[p, way])

    def ag1_wait(yr):
        for p in range(PARTS):
            for way in range(2):
                ag_wait(p, shards[p, yr, 2, 0], way, key_1(p, yr, 1, way))

    def ag2_first(g):
        for p in range(PARTS):
            for way in range(2):
                ag_send(p, shards[p, g[0], g[1], 0], None, key_2(p, g, 0, way), peers2[p, way])

    def ag2_next(g):
        for p in range(PARTS):
            for way in range(2):
                s = shards[p, g[0], g[1], 3 if way == 0 else 1]
                ag_wait(p, s, None, key_2(p, g, 0, way))
                ag_send(p, s, way, key_2(p, g, 1, way), peers2[p, way])

    def ag2_wait(g):
        for p in range(PARTS):
            for way in range(2):
                ag_wait(p, shards[p, g[0], g[1], 2], way, key_2(p, g, 1, way))

    def prow(p, s, h, n):
        return pl.ds(pl.multiple_of(s * KV + p * 512 + h * 256, 256), n)

    def slot(p, stage, g, way):
        k = (g[0] * 4 + g[1]) if stage == 1 else 8 + g
        return (p * 10 + k) * 2 + way

    def rs_key(p, stage, g, step, way):
        return key_2(p, g, step, way) if stage == 1 else key_1(p, g, step, way)

    def rs_shard(p, stage, g, o):
        return shards[p, g[0], g[1], o] if stage == 1 else shards[p, g, o, 0]

    def rs_peer(p, stage, way):
        return peers2[p, way] if stage == 1 else peers1[p, way]

    def rs_first(stage, g):
        for p in range(PARTS):
            for way in range(2):
                k = rs_key(p, stage, g, 0, way)
                s = slot(p, stage, g, way)
                remote(
                    pt.at[prow(p, rs_shard(p, stage, g, 2), way, 256)],
                    x1.at[pl.ds(s * 256, 256)],
                    rs_s.at[k],
                    rs_r.at[k],
                    (rep, rs_peer(p, stage, way)),
                ).start()

    def rs_next(stage, g):
        for p in range(PARTS):
            for way in range(2):
                k = rs_key(p, stage, g, 0, way)
                s = slot(p, stage, g, way)
                ref = x1.at[pl.ds(s * 256, 256)]
                remote(ref, ref, rs_s.at[k], rs_r.at[k], (rep, ypeer)).wait_recv()
                to = rs_shard(p, stage, g, 1 if way == 0 else 3)
                r = prow(p, to, way, 256)
                pt[r, :] = (pt[r, :].astype(F32) + x1[pl.ds(s * 256, 256), :].astype(F32)).astype(BF)
                k = rs_key(p, stage, g, 1, way)
                remote(
                    pt.at[prow(p, to, 0, 512)],
                    x2.at[pl.ds(s * 512, 512)],
                    rs_s.at[k],
                    rs_r.at[k],
                    (rep, rs_peer(p, stage, way)),
                ).start()

    def rs_last(stage, g):
        for p in range(PARTS):
            for way in range(2):
                k = rs_key(p, stage, g, 1, way)
                ref = x2.at[pl.ds(slot(p, stage, g, way) * 512, 512)]
                remote(ref, ref, rs_s.at[k], rs_r.at[k], (rep, ypeer)).wait_recv()
            r = prow(p, rs_shard(p, stage, g, 0), 0, 512)
            a = x2[pl.ds(slot(p, stage, g, 0) * 512, 512), :].astype(F32)
            b = x2[pl.ds(slot(p, stage, g, 1) * 512, 512), :].astype(F32)
            pt[r, :] = (pt[r, :].astype(F32) + (a + b)).astype(BF)

    def rs_y_send():
        for p in range(PARTS):
            k = key_y(p)
            remote(
                pt.at[prow(p, ypeer, 0, 512)],
                ybuf.at[pl.ds(p * 512, 512)],
                rs_s.at[k],
                rs_r.at[k],
                (rep, ypeer),
            ).start()

    def rs_y_wait():
        for p in range(PARTS):
            k = key_y(p)
            ref = ybuf.at[pl.ds(p * 512, 512)]
            remote(ref, ref, rs_s.at[k], rs_r.at[k], (rep, ypeer)).wait_recv()

    def gain_ref(stage, yr, off):
        if stage == 0:
            return gbuf.at[at(yr, 0, off)]
        if stage == 1:
            return gbuf.at[pl.ds(at(yr, off, 0) // 4 * 4, 4)]
        return gbuf.at[pl.ds(at(yr, 0, 0) // 16 * 16, 16)]

    def gain_send(stage):
        for o in (1, 2, 3) if stage < 2 else (0,):
            k = stage * 3 + max(o, 1) - 1
            ref = gain_ref(stage, 0, 0)
            remote(ref, ref, g_s.at[k], g_r.at[k], (rep, gpeers[k])).start()

    def gain_wait(stage):
        for o in (1, 2, 3) if stage < 2 else (0,):
            k = stage * 3 + max(o, 1) - 1
            ref = gain_ref(stage, 0, 4 - o) if stage < 2 else gain_ref(2, 1, 0)
            remote(ref, ref, g_s.at[k], g_r.at[k], (rep, ypeer)).wait_recv()

    def ps_send(k):
        if k == 0:
            src, dst, dev = ps.at[pl.ds(other, half)], psr, (twin, me)
        elif k == 1:
            src, dst, dev = psum, srecv, (across, me)
        else:
            src, dst, dev = ps.at[pl.ds(mine, half)], trecv, (twin, me)
        remote(src, dst, p_s.at[k], p_r.at[k], dev).start()

    def ps_wait(k):
        ref = (psr, srecv, trecv)[k]
        remote(ref, ref, p_s.at[k], p_r.at[k], (twin, me)).wait_recv()

    def ps_sent(k):
        ref = (psr, srecv, trecv)[k]
        remote(ref, ref, p_s.at[k], p_r.at[k], (twin, me)).wait_send()

    loads["w"].wait()
    ag1_first(0)
    ag_y_send()
    ag2_first((0, 0))
    loads["gain"].wait()
    gain_send(0)
    loads["ps"].wait()
    ps_send(0)

    loads["ct"].wait()
    loads["cos"].wait()
    loads["sin"].wait()

    @pl.loop(0, 4)
    def _(h):
        cols = pl.ds(pl.multiple_of(h * HEAD, HEAD), HEAD)
        v = kv[:, cols].astype(F32)
        r = (v * cos_v[...] - pltpu.roll(v, HEAD // 2, 1) * sin_v[...]).astype(BF)
        kv[:, cols] = r
        kvt[cols, :] = r.T

    @pl.loop(4, 8)
    def _(h):
        cols = pl.ds(pl.multiple_of(h * HEAD, HEAD), HEAD)
        kvt[cols, :] = kv[:, cols].T

    gain_wait(0)
    gain_send(1)
    ag1_next(0)

    ps_wait(0)
    ps_sent(0)

    @pl.loop(0, 12)
    def _(i):
        r = pl.ds(pl.multiple_of(i * 16, 16), 16)
        rm = pl.ds(pl.multiple_of(mine + i * 16, 16), 16)
        psum[r, :] = ps[rm, :] + psr[r, :]

    ps_send(1)
    gain_wait(1)
    gain_send(2)

    ag_y_wait()
    ag1_first(1)
    ag2_first((0, 3))
    ag2_first((0, 1))

    gain_wait(2)
    for j in range(32):
        grow[:, j * 128 : (j + 1) * 128] = jnp.broadcast_to(gbuf[j], (8, 128))
    loads["x"].wait()

    @pl.loop(0, TOK // 16)
    def _(i):
        r = pl.ds(pl.multiple_of(i * 16, 16), 16)
        v = x_v[r, :].astype(F32)
        inv = lax.rsqrt(jnp.mean(v * v, axis=-1, keepdims=True) + epsilon)
        invb[r, :] = jnp.broadcast_to(inv, (16, 128))
        hid[r, :] = (x_v[r, :].astype(F32) * inv * grow[0:1, :]).astype(BF)

    def ag_a():
        ag2_next((0, 0))
        ag2_first((1, 0))

    def ag_b():
        ag1_next(1)

    def ag_c():
        ag2_next((0, 3))
        ag1_wait(0)
        ag2_first((0, 2))

    def ag_d():
        ag2_next((0, 1))
        ag2_first((1, 3))

    def ag_e():
        ag2_next((1, 0))
        ag2_first((1, 1))

    steps = {0: ag_a, 3: ag_b, 6: ag_c, 9: ag_d, 12: ag_e}

    @pl.loop(0, 16)
    def _(i):
        for k, fn in steps.items():
            pl.when(i == k)(fn)
        res = jnp.dot(
            kvt[...],
            hid[:, pl.ds(pl.multiple_of(i * 256, 256), 256)],
            preferred_element_type=F32,
        )
        r0 = pl.multiple_of(i * 2048, 2048)
        pt[pl.ds(r0, 1024), :] = res[:, :128].astype(BF)
        pt[pl.ds(r0 + 1024, 1024), :] = res[:, 128:].astype(BF)

    ag1_wait(1)
    ag2_first((1, 2))
    ag2_next((0, 2))

    ps_wait(1)
    ps_sent(1)

    @pl.loop(0, 12)
    def _(i):
        r = pl.ds(pl.multiple_of(i * 16, 16), 16)
        rm = pl.ds(pl.multiple_of(mine + i * 16, 16), 16)
        ps[rm, :] = psum[r, :] + srecv[r, :]

    ps_send(2)
    ag2_next((1, 3))
    ag2_next((1, 1))
    ps_wait(2)
    ps_sent(2)
    loads["om"].wait()
    loads["gp"].wait()
    loads["lp"].wait()

    def update(r, total):
        average = total * 0.25
        m = momentum_rate * om[r, :] + average
        gn = gp[r, :] - outer_rate * (average + momentum_rate * m)
        mom_out[r, :] = m
        glob_out[r, :] = gn
        loc_out[r, :] = (mixing_rate * lp[r, :].astype(F32) + (1.0 - mixing_rate) * gn).astype(BF)

    @pl.loop(0, 12)
    def _(i):
        rm = pl.ds(pl.multiple_of(mine + i * 16, 16), 16)
        update(rm, ps[rm, :])
        ro = pl.ds(pl.multiple_of(other + i * 16, 16), 16)
        update(ro, trecv[pl.ds(pl.multiple_of(i * 16, 16), 16), :])

    ag2_next((1, 2))
    order = SCATTER_ORDER
    rs_first(1, order[0])
    rs_first(1, order[1])
    for yr in range(2):
        for o in range(4):
            ag2_wait((yr, o))

    def r0():
        rs_first(1, order[2])
        rs_next(1, order[0])

    def r1():
        rs_first(1, order[3])
        rs_next(1, order[1])

    def r2():
        rs_first(1, order[4])
        rs_next(1, order[2])

    def r2b():
        rs_last(1, order[0])
        rs_first(2, 1)

    def r3():
        rs_first(1, order[5])
        rs_next(1, order[3])
        rs_last(1, order[1])

    def r4():
        rs_first(1, order[6])
        rs_next(1, order[4])

    def r4b():
        rs_last(1, order[2])
        rs_next(2, 1)

    def r5():
        rs_first(1, order[7])
        rs_next(1, order[5])
        rs_last(1, order[3])

    def r6():
        rs_next(1, order[6])
        rs_last(1, order[4])
        rs_first(2, 0)

    def r6b():
        rs_last(2, 1)
        rs_y_send()

    def r7():
        rs_next(1, order[7])
        rs_last(1, order[5])

    def r8():
        rs_last(1, order[6])
        rs_next(2, 0)

    def r9():
        rs_last(1, order[7])

    cb[...] = jnp.zeros_like(cb)
    fwd_steps = {0: r0, 1: r1, 2: r2, 3: r2b}

    @pl.loop(0, 4)
    def _(n):
        for k, fn in fwd_steps.items():
            pl.when(n == k)(fn)
        cols = pl.ds(pl.multiple_of(n * 256, 256), 256)
        pre[...] = jnp.dot(hid[...], wbuf[:, cols], preferred_element_type=F32)
        for b in range(2):
            c128 = pl.ds(pl.multiple_of(n * 256 + b * 128, 128), 128)
            v = pre[:, b * 128 : (b + 1) * 128]
            cb[...] += v * kv[:, c128].astype(F32)

            @pl.when(n < 2)
            def _():
                v = pre[:, b * 128 : (b + 1) * 128]
                kv_out[:, c128] = (v * cos_v[...] + pltpu.roll(v, HEAD // 2, 1) * sin_v[...]).astype(BF)

            @pl.when(n >= 2)
            def _():
                kv_out[:, c128] = pre[:, b * 128 : (b + 1) * 128].astype(BF)

    cb[...] = jnp.broadcast_to(jnp.sum(cb[...], axis=-1, keepdims=True) * (1.0 / D), (TOK, 128))

    bwd_steps = {0: r3, 2: r4, 4: r4b, 5: r5, 8: r6, 10: r6b, 12: r7, 15: r8}

    @pl.loop(0, 16)
    def _(i):
        for k, fn in bwd_steps.items():
            pl.when(i == k)(fn)
        rows = pl.ds(pl.multiple_of(i * 256, 256), 256)
        pre[...] = lax.dot_general(
            kv[...], wbuf[rows, :], (((1,), (1,)), ((), ())), preferred_element_type=F32
        )
        for b in range(2):
            cols = pl.ds(pl.multiple_of(i * 256 + b * 128, 128), 128)
            inv = invb[...]
            normed = x_v[:, cols].astype(F32) * inv
            ng = pre[:, b * 128 : (b + 1) * 128] * grow[0:1, cols]
            ig_out[:, cols] = (inv * (ng - normed * cb[...])).astype(BF)

    r9()
    rs_last(2, 0)
    rs_y_wait()
    scale = 1.0 / math.sqrt(TOK * 32)
    acc = jnp.zeros((128, 128), F32)
    for k in range(8):
        r = pl.ds(pl.multiple_of(me * KV + k * 128, 128), 128)
        t = ((pt[r, :].astype(F32) + ybuf[k * 128 : (k + 1) * 128, :].astype(F32)) * scale).T
        wg_out[:, k * 128 : (k + 1) * 128] = t
        acc = acc + t * wbuf[pl.ds(own_rows, ROWS), k * 128 : (k + 1) * 128].astype(F32)
    gg_out[...] = jnp.sum(acc.T, axis=0, keepdims=True) / gbuf[me]

    def done(ref, sem):
        remote(ref, ref, sem, g_r.at[0], (rep, ypeer)).wait_send()

    for p in range(PARTS):
        done(wbuf.at[pl.ds(0, 64)], ag_s.at[key_y(p)])
        done(ybuf.at[pl.ds(0, 512)], rs_s.at[key_y(p)])
        for step in range(2):
            for way in range(2):
                keys = [key_1(p, yr, step, way) for yr in range(2)]
                keys += [key_2(p, (yr, o), step, way) for yr in range(2) for o in range(4)]
                for k in keys:
                    done(wbuf.at[pl.ds(0, 32 if step else 64)], ag_s.at[k])
                    done(ybuf.at[pl.ds(0, 512 if step else 256)], rs_s.at[k])
    for k in range(7):
        done(gain_ref(k // 3, 0, 0), g_s.at[k])


def local(
    layer_input,
    norm_gain,
    kv_weight,
    kv_cotangent,
    pseudo_grad,
    outer_momentum,
    global_params,
    local_params,
):
    positions = (lax.axis_index("fsdp") * TOK + jnp.arange(TOK, dtype=jnp.int32)) % SEQ_LEN
    lane = jnp.arange(HEAD, dtype=jnp.int32)
    index_f = (lane % (HEAD // 2)).astype(F32)
    inverse = jnp.exp(index_f * (-2.0 * math.log(rope_base) / HEAD))
    angle = positions.astype(F32)[:, None] * inverse[None, :]
    cosine = jnp.cos(angle)
    sine = jnp.sin(angle) * jnp.where(lane < HEAD // 2, -1.0, 1.0)[None, :]
    any_spec = pl.BlockSpec(memory_space=pl.ANY)
    vmem = pl.BlockSpec(memory_space=pltpu.VMEM)
    dma = pltpu.SemaphoreType.DMA
    outs = pl.pallas_call(
        kernel,
        out_shape=(
            jax.ShapeDtypeStruct((TOK, KV), BF),
            jax.ShapeDtypeStruct((TOK, D), BF),
            jax.ShapeDtypeStruct((ROWS, KV), F32),
            jax.ShapeDtypeStruct((1, ROWS), F32),
            jax.ShapeDtypeStruct((PSR, KV), F32),
            jax.ShapeDtypeStruct((PSR, KV), F32),
            jax.ShapeDtypeStruct((PSR, KV), BF),
        ),
        in_specs=[any_spec] * 10,
        out_specs=(vmem,) * 7,
        scratch_shapes=[
            pltpu.VMEM((TOK, D), BF),
            pltpu.VMEM((TOK, D), BF),
            pltpu.VMEM((D, KV), BF),
            pltpu.VMEM((TOK, KV), BF),
            pltpu.VMEM((KV, TOK), BF),
            pltpu.VMEM((32 * KV, ROWS), BF),
            pltpu.VMEM((40 * 256, ROWS), BF),
            pltpu.VMEM((40 * 512, ROWS), BF),
            pltpu.VMEM((KV, ROWS), BF),
            pltpu.VMEM((32, 1, ROWS), F32),
            pltpu.VMEM((8, D), F32),
            pltpu.VMEM((TOK, 128), F32),
            pltpu.VMEM((TOK, 128), F32),
            pltpu.VMEM((TOK, 256), F32),
            pltpu.VMEM((TOK, 128), F32),
            pltpu.VMEM((TOK, 128), F32),
            pltpu.VMEM((PSR, KV), F32),
            pltpu.VMEM((PSR // 2, KV), F32),
            pltpu.VMEM((PSR // 2, KV), F32),
            pltpu.VMEM((PSR // 2, KV), F32),
            pltpu.VMEM((PSR // 2, KV), F32),
            pltpu.VMEM((PSR, KV), F32),
            pltpu.VMEM((PSR, KV), F32),
            pltpu.VMEM((PSR, KV), BF),
            dma((10,)),
            dma((2 * PER_PART,)),
            dma((2 * PER_PART,)),
            dma((2 * PER_PART,)),
            dma((2 * PER_PART,)),
            dma((7,)),
            dma((7,)),
            dma((3,)),
            dma((3,)),
        ],
        compiler_params=pltpu.CompilerParams(
            collective_id=0, has_side_effects=True, vmem_limit_bytes=63 * 1024 * 1024
        ),
    )(
        layer_input[0],
        norm_gain.astype(F32),
        kv_weight[0],
        kv_cotangent[0],
        pseudo_grad[0],
        outer_momentum,
        global_params,
        local_params[0],
        cosine,
        sine,
    )
    kv_out, input_grad, weight_grad, gain_grad, momentum_new, global_new, local_new = outs
    return (
        kv_out[None],
        input_grad[None],
        weight_grad[None],
        gain_grad,
        momentum_new,
        global_new,
        local_new[None],
    )


def solution(mesh):
    shared = P("replica", "fsdp", None)
    in_specs = (
        shared,
        P("replica", "fsdp"),
        shared,
        shared,
        shared,
        P("fsdp", None),
        P("fsdp", None),
        shared,
    )
    out_specs = (
        shared,
        shared,
        shared,
        P("replica", "fsdp"),
        P("fsdp", None),
        P("fsdp", None),
        shared,
    )
    return jax.shard_map(local, mesh=mesh, in_specs=in_specs, out_specs=out_specs, check_vma=False)
```

time: 416 us -> 132 us (0.32)
  blocking collectives: 241 us -> 0 us
  Pallas kernels: 0 us -> 116 us
  waiting for transfers between devices: 99.4 us -> 0 us
  matrix products: 30.1 us -> 0 us
  other arithmetic: 23.1 us -> 3.01 us
  between operations: 16.3 us -> 0.65 us
  local copies, waits for them, and re-layouts: 5.51 us -> 13 us
    unnamed x1 -> x0, blocking collectives: 158 us -> none
    pallas_call x0 -> x1, Pallas kernels: none -> 116 us  [local(): pl.pallas_call(kernel, out_shape=(jax.ShapeDtypeStruct((TOK, KV), BF), ja...]
    all_gather x1 -> x0, blocking collectives: 82.9 us -> none  [local(): lax.all_gather(gain_shard, 'fsdp', axis=0, tiled=True)]
    all_gather x1 -> x0, waiting for transfers between devices: 80.9 us -> none  [local(): lax.all_gather(weight_shard, 'fsdp', axis=0, tiled=True)]
    dot_general x3 -> x0, matrix products: 30.1 us -> none  [the longest x1 13.6 us: backward_piece(): lax.dot_general(kv_grad, weight_piece, (((1,), (1,)), ((), ())), preferre...]
    reduce_scatter x1 -> x0, waiting for transfers between devices: 17.3 us -> none  [local(): lax.psum_scatter(weight_term, 'fsdp', scatter_dimension=0, tiled=True)]
    broadcast_in_dim x2 -> x0, other arithmetic: 11.9 us -> none  [the longest x1 7.32 us: local(): input_grad[None]]
    unnamed x20 -> x17, local copies, waits for them, and re-layouts: 2.63 us -> 13 us
  transfers between devices with their start and end apart: 3 -> 0, of which waited for: 2 -> 0; matrix products, arithmetic and copies ran while one was open for 14% -> 0% of each run, Pallas kernels for 0% -> 0%
where the time goes in v1:
time: 132 us
  Pallas kernels  116 us (88%)
  local copies, waits for them, and re-layouts  13 us (10%)
  other arithmetic  3.01 us (2%)
    pallas_call x1, Pallas kernels, local(): pl.pallas_call(kernel, out_shape=(jax.ShapeDtypeStruct((TOK, KV), BF), ja...  116 us
    unnamed x17, local copies, waits for them, and re-layouts  13 us

profile of v1, /device:TPU:0, one launch (start us, length us, event | category | flops | bytes accessed | tf_op | source)
XLA Modules:
  0.0 132.1 jit_solution(18080959472862406511)
XLA Ops:
  0.6 1.2 convert_element_type.17.gain_hbm
  1.8 1.8 %fusion = (f32[512,128]{1,0:T(8,128)}, f32[512,128]{1,0:T(8,128)}) fusion(f32[128]{0:T(128)S(1)} %get-tuple-element.23, f32[128]{0:T(128)S(1)} %get-tuple-element.24, f32[512]{0:T(512)S(1)} %fusion.2), kind=kLoop, calls=%fused_computation.2 | loop fusion | flops 131072 | bytes 527360 | tf_op jit(solution)/shard_map/mul | solution.py:610
  3.6 115.5 %shard_map.135 = (bf16[512,1024]{1,0:T(8,128)(2,1)}, bf16[512,4096]{1,0:T(8,128)(2,1)}, f32[128,1024]{1,0:T(8,128)}, f32[1,128]{1,0:T(1,128)}, f32[384,1024]{1,0...) custom-call(bf16[512,4096]{1,0:T(8,128)(2,1)} %bitcast.9, f32[1,128]{1,0:T(1,128)} %convert_element_type.17.gain_hbm, ...), custom_call_target="tpu_custom_call" | custom-call | tf_op jit(solution)/shard_map/pallas_call | solution.py:614
  119.2 2.3 %copy.22 = bf16[1,512,1024]{2,1,0:T(8,128)(2,1)} copy(bf16[1,512,1024]{2,1,0:T(8,128)(2,1)} %bitcast.13) | data formatting | bytes 2097152
  121.4 0.0 copy-start.3
  121.4 0.0 copy-start.4
  121.4 0.0 copy-start.1
  121.4 4.8 %copy.23 = bf16[1,512,4096]{2,1,0:T(8,128)(2,1)} copy(bf16[1,512,4096]{2,1,0:T(8,128)(2,1)} %bitcast.10) | data formatting | bytes 8388608
  126.3 0.0 copy-done.3
  126.3 0.8 copy.24
  127.1 0.0 copy-done.4
  127.1 0.5 copy.25
  127.6 0.0 copy-done.1
  127.6 0.0 copy-start
  127.6 1.1 copy.26
  128.7 0.8 copy-done
  129.6 0.0 copy-start.2
  129.6 1.1 copy.27
  130.7 0.5 copy-done.2
  131.3 0.9 copy.28
  (2 shorter events, 0.0 us)
Async XLA Ops:
  121.4 4.9 %copy-start.3 = (f32[128,1024]{1,0:T(8,128)S(1)}, f32[128,1024]{1,0:T(8,128)}, u32[]{:S(2)}) copy-start(f32[128,1024]{1,0:T(8,128)} %get-tuple-element.16) | copy-start | bytes 1572868
  121.4 5.6 %copy-start.4 = (f32[1,128]{1,0:T(1,128)S(1)}, f32[1,128]{1,0:T(1,128)}, u32[]{:S(2)}) copy-start(f32[1,128]{1,0:T(1,128)} %get-tuple-element.35) | copy-start | bytes 1540
  121.4 6.2 %copy-start.1 = (f32[384,1024]{1,0:T(8,128)S(1)}, f32[384,1024]{1,0:T(8,128)}, u32[]{:S(2)}) copy-start(f32[384,1024]{1,0:T(8,128)} %get-tuple-element.36) | copy-start | bytes 4718596
  127.6 2.0 %copy-start = (f32[384,1024]{1,0:T(8,128)S(1)}, f32[384,1024]{1,0:T(8,128)}, u32[]{:S(2)}) copy-start(f32[384,1024]{1,0:T(8,128)} %get-tuple-element.37) | copy-start | bytes 4718596
  129.6 1.7 %copy-start.2 = (bf16[384,1024]{1,0:T(8,128)(2,1)S(1)}, bf16[384,1024]{1,0:T(8,128)(2,1)}, u32[]{:S(2)}) copy-start(bf16[384,1024]{1,0:T(8,128)(2,1)} %get-tuple-element.20) | copy-start | bytes 2359300

commit v2 on v1

--- a/solution.py
+++ b/solution.py
@@ -22,6 +22,9 @@
 outer_rate = 0.7
 mixing_rate = 0.5
 
+TURN_MID = 507 / 262144
+TURN_LOW = 2 * math.pi - 6.28125 - TURN_MID
+
 MESH = pl.DeviceIdType.MESH
 BF = jnp.bfloat16
 F32 = jnp.float32
@@ -44,15 +47,13 @@
 
 def kernel(
     x_hbm,
-    gain_hbm,
+    gain_v,
     w_hbm,
     ct_hbm,
     ps_hbm,
     om_hbm,
     gp_hbm,
     lp_hbm,
-    cos_hbm,
-    sin_hbm,
     kv_out,
     ig_out,
     wg_out,
@@ -135,16 +136,14 @@
 
     own_rows = pl.multiple_of(me * ROWS, ROWS)
     load("w", w_hbm, wbuf.at[pl.ds(own_rows, ROWS)], 0)
-    load("gain", gain_hbm, gbuf.at[me], 1)
     load("ps", ps_hbm, ps, 2)
     load("ct", ct_hbm, kv, 3)
-    load("cos", cos_hbm, cos_v, 4)
-    load("sin", sin_hbm, sin_v, 5)
     load("x", x_hbm, x_v, 6)
     load("om", om_hbm, om, 7)
     load("gp", gp_hbm, gp, 8)
     load("lp", lp_hbm, lp, 9)
 
+    gbuf[me] = gain_v[...].astype(F32)
     barrier = pltpu.get_barrier_semaphore()
     greet = [(rep, d) for d in gpeers] + [(twin, me), (across, me)]
     for dev in greet:
@@ -329,14 +328,26 @@
     ag1_first(0)
     ag_y_send()
     ag2_first((0, 0))
-    loads["gain"].wait()
-    gain_send(0)
     loads["ps"].wait()
     ps_send(0)
+    gain_send(0)
+
+    lane = lax.broadcasted_iota(jnp.int32, (8, HEAD), 1)
+    inverse = jnp.exp((lane % (HEAD // 2)).astype(F32) * (-2.0 * math.log(rope_base) / HEAD))
+    sign = jnp.where(lane < HEAD // 2, -1.0, 1.0)
+    first_position = (me * TOK) % SEQ_LEN
+
+    @pl.loop(0, TOK // 8)
+    def _(i):
+        r = pl.ds(pl.multiple_of(i * 8, 8), 8)
+        position = first_position + i * 8 + lax.broadcasted_iota(jnp.int32, (8, HEAD), 0)
+        angle = position.astype(F32) * inverse
+        turns = jnp.round(angle * (0.5 / math.pi))
+        angle = ((angle - turns * 6.28125) - turns * TURN_MID) - turns * TURN_LOW
+        cos_v[r, :] = jnp.cos(angle)
+        sin_v[r, :] = jnp.sin(angle) * sign
 
     loads["ct"].wait()
-    loads["cos"].wait()
-    loads["sin"].wait()
 
     @pl.loop(0, 4)
     def _(h):
@@ -591,6 +602,15 @@
         done(gain_ref(k // 3, 0, 0), g_s.at[k])
 
 
+def write_kernel(*refs):
+    n = len(refs) // 2
+    copies = [pltpu.make_async_copy(refs[k], refs[n + k], refs[2 * n].at[k]) for k in range(n)]
+    for c in copies:
+        c.start()
+    for c in copies:
+        c.wait()
+
+
 def local(
     layer_input,
     norm_gain,
@@ -601,28 +621,21 @@
     global_params,
     local_params,
 ):
-    positions = (lax.axis_index("fsdp") * TOK + jnp.arange(TOK, dtype=jnp.int32)) % SEQ_LEN
-    lane = jnp.arange(HEAD, dtype=jnp.int32)
-    index_f = (lane % (HEAD // 2)).astype(F32)
-    inverse = jnp.exp(index_f * (-2.0 * math.log(rope_base) / HEAD))
-    angle = positions.astype(F32)[:, None] * inverse[None, :]
-    cosine = jnp.cos(angle)
-    sine = jnp.sin(angle) * jnp.where(lane < HEAD // 2, -1.0, 1.0)[None, :]
     any_spec = pl.BlockSpec(memory_space=pl.ANY)
     vmem = pl.BlockSpec(memory_space=pltpu.VMEM)
     dma = pltpu.SemaphoreType.DMA
     outs = pl.pallas_call(
         kernel,
         out_shape=(
-            jax.ShapeDtypeStruct((TOK, KV), BF),
-            jax.ShapeDtypeStruct((TOK, D), BF),
-            jax.ShapeDtypeStruct((ROWS, KV), F32),
-            jax.ShapeDtypeStruct((1, ROWS), F32),
-            jax.ShapeDtypeStruct((PSR, KV), F32),
-            jax.ShapeDtypeStruct((PSR, KV), F32),
-            jax.ShapeDtypeStruct((PSR, KV), BF),
+            pltpu.VMEM((TOK, KV), BF),
+            pltpu.VMEM((TOK, D), BF),
+            pltpu.VMEM((ROWS, KV), F32),
+            pltpu.VMEM((1, ROWS), F32),
+            pltpu.VMEM((PSR, KV), F32),
+            pltpu.VMEM((PSR, KV), F32),
+            pltpu.VMEM((PSR, KV), BF),
         ),
-        in_specs=[any_spec] * 10,
+        in_specs=[any_spec, vmem] + [any_spec] * 6,
         out_specs=(vmem,) * 7,
         scratch_shapes=[
             pltpu.VMEM((TOK, D), BF),
@@ -660,20 +673,26 @@
             dma((3,)),
         ],
         compiler_params=pltpu.CompilerParams(
-            collective_id=0, has_side_effects=True, vmem_limit_bytes=63 * 1024 * 1024
+            collective_id=0, has_side_effects=True, vmem_limit_bytes=50 * 1024 * 1024
         ),
     )(
         layer_input[0],
-        norm_gain.astype(F32),
+        norm_gain,
         kv_weight[0],
         kv_cotangent[0],
         pseudo_grad[0],
         outer_momentum,
         global_params,
         local_params[0],
-        cosine,
-        sine,
     )
+    outs = pl.pallas_call(
+        write_kernel,
+        out_shape=tuple(jax.ShapeDtypeStruct(o.shape, o.dtype) for o in outs),
+        in_specs=[vmem] * 7,
+        out_specs=(any_spec,) * 7,
+        scratch_shapes=[dma((7,))],
+        compiler_params=pltpu.CompilerParams(vmem_limit_bytes=1024 * 1024),
+    )(*outs)
     kv_out, input_grad, weight_grad, gain_grad, momentum_new, global_new, local_new = outs
     return (
         kv_out[None],

time: 132 us -> 117 us (0.89)
  local copies, waits for them, and re-layouts: 13 us -> 0 us
  other arithmetic: 3.01 us -> 0 us
    unnamed x17 -> x0, local copies, waits for them, and re-layouts: 13 us -> none
    mul x1 -> x0, other arithmetic: 1.83 us -> none  [local(): sine = jnp.sin(angle) * jnp.where(lane < HEAD // 2, -1.0, 1.0)[None, :]]
    pallas_call x1 -> x2, Pallas kernels: 116 us -> 116 us  [the longest x1 113 us: local(): pl.pallas_call(kernel, out_shape=(pltpu.VMEM((TOK, KV), BF), pltpu.VMEM((...]
where the time goes in v2:
time: 117 us
  Pallas kernels  116 us (99%)
    pallas_call x1, Pallas kernels, local(): pl.pallas_call(kernel, out_shape=(pltpu.VMEM((TOK, KV), BF), pltpu.VMEM((...  113 us
    pallas_call x1, Pallas kernels, local(): pl.pallas_call(write_kernel, out_shape=tuple((jax.ShapeDtypeStruct(o.shap...  3.78 us

profile of v2, /device:TPU:0, one launch (start us, length us, event | category | flops | bytes accessed | tf_op | source)
XLA Modules:
  0.0 116.9 jit_solution(6777411010394564746)
XLA Ops:
  0.6 112.5 %shard_map.135 = (bf16[512,1024]{1,0:T(8,128)(2,1)S(1)}, bf16[512,4096]{1,0:T(8,128)(2,1)S(1)}, f32[128,1024]{1,0:T(8,128)S(1)}, f32[1,128]{1,0:T(1,128)S(1)}, f...) custom-call(bf16[512,4096]{1,0:T(8,128)(2,1)} %bitcast.9, bf16[1,128]{1,0:T(2,128)(2,1)} %gain_v.1, ...), custom_call_target="tpu_custom_call" | custom-call | tf_op jit(solution)/shard_map/pallas_call | solution.py:627
  113.2 3.8 %shard_map.136 = (bf16[512,1024]{1,0:T(8,128)(2,1)}, bf16[512,4096]{1,0:T(8,128)(2,1)}, f32[128,1024]{1,0:T(8,128)}, f32[1,128]{1,0:T(1,128)}, f32[384,1024]{1,0...) custom-call(bf16[512,1024]{1,0:T(8,128)(2,1)S(1)} %get-tuple-element.21.refs_0_, ...), custom_call_target="tpu_custom_call" | custom-call | tf_op jit(solution)/shard_map/pallas_call | solution.py:688

commit v3 on v2

--- a/solution.py
+++ b/solution.py
@@ -43,6 +43,12 @@
 
 def key_2(p, g, step, way):
     return p * PER_PART + 9 + (g[0] * 4 + g[1]) * 4 + step * 2 + way
+
+
+def turn(angle):
+    turns = jnp.round(angle * (0.5 / math.pi))
+    angle = ((angle - turns * 6.28125) - turns * TURN_MID) - turns * TURN_LOW
+    return jnp.cos(angle), jnp.sin(angle)
 
 
 def kernel(
@@ -325,27 +331,28 @@
         remote(ref, ref, p_s.at[k], p_r.at[k], (twin, me)).wait_send()
 
     loads["w"].wait()
+    gain_send(0)
     ag1_first(0)
     ag_y_send()
-    ag2_first((0, 0))
     loads["ps"].wait()
     ps_send(0)
-    gain_send(0)
-
-    lane = lax.broadcasted_iota(jnp.int32, (8, HEAD), 1)
+
+    lane = lax.broadcasted_iota(jnp.int32, (64, HEAD), 1)
     inverse = jnp.exp((lane % (HEAD // 2)).astype(F32) * (-2.0 * math.log(rope_base) / HEAD))
+    small = lax.broadcasted_iota(jnp.int32, (64, HEAD), 0).astype(F32) * inverse
+    position = (me * TOK) % SEQ_LEN + 64 * lax.broadcasted_iota(jnp.int32, (8, HEAD), 0)
+    base = position.astype(F32) * inverse[:8]
+    cos_0, sin_0 = turn(small)
+    cos_b, sin_b = turn(base)
     sign = jnp.where(lane < HEAD // 2, -1.0, 1.0)
-    first_position = (me * TOK) % SEQ_LEN
-
-    @pl.loop(0, TOK // 8)
-    def _(i):
-        r = pl.ds(pl.multiple_of(i * 8, 8), 8)
-        position = first_position + i * 8 + lax.broadcasted_iota(jnp.int32, (8, HEAD), 0)
-        angle = position.astype(F32) * inverse
-        turns = jnp.round(angle * (0.5 / math.pi))
-        angle = ((angle - turns * 6.28125) - turns * TURN_MID) - turns * TURN_LOW
-        cos_v[r, :] = jnp.cos(angle)
-        sin_v[r, :] = jnp.sin(angle) * sign
+    for b in range(8):
+        cb_row, sb_row = cos_b[b : b + 1], sin_b[b : b + 1]
+        cos_v[b * 64 : (b + 1) * 64, :] = cos_0 * cb_row - sin_0 * sb_row
+        sin_v[b * 64 : (b + 1) * 64, :] = (sin_0 * cb_row + cos_0 * sb_row) * sign
+
+    gain_wait(0)
+    gain_send(1)
+    ag2_first((0, 0))
 
     loads["ct"].wait()
 
@@ -357,67 +364,82 @@
         kv[:, cols] = r
         kvt[cols, :] = r.T
 
+    ag1_next(0)
+    ag2_first((0, 3))
+    ag2_first((0, 1))
+
     @pl.loop(4, 8)
     def _(h):
         cols = pl.ds(pl.multiple_of(h * HEAD, HEAD), HEAD)
         kvt[cols, :] = kv[:, cols].T
 
-    gain_wait(0)
-    gain_send(1)
-    ag1_next(0)
+    gain_wait(1)
+    gain_send(2)
+    ag_y_wait()
+    ag1_first(1)
+    ag2_next((0, 0))
+    ag1_wait(0)
+    ag2_first((1, 0))
+    ag2_first((0, 2))
 
     ps_wait(0)
     ps_sent(0)
 
-    @pl.loop(0, 12)
+    @pl.loop(0, 4)
     def _(i):
-        r = pl.ds(pl.multiple_of(i * 16, 16), 16)
-        rm = pl.ds(pl.multiple_of(mine + i * 16, 16), 16)
-        psum[r, :] = ps[rm, :] + psr[r, :]
-
+        r = pl.ds(pl.multiple_of(i * 48, 16), 48)
+        rm = pl.ds(pl.multiple_of(mine + i * 48, 16), 48)
+        psum[r, :] = (ps[rm, :] + psr[r, :]).astype(BF)
+
+    gain_wait(2)
     ps_send(1)
-    gain_wait(1)
-    gain_send(2)
-
-    ag_y_wait()
-    ag1_first(1)
-    ag2_first((0, 3))
-    ag2_first((0, 1))
-
-    gain_wait(2)
     for j in range(32):
         grow[:, j * 128 : (j + 1) * 128] = jnp.broadcast_to(gbuf[j], (8, 128))
     loads["x"].wait()
 
+    @pl.loop(0, TOK // 64)
+    def _(i):
+        r = pl.ds(pl.multiple_of(i * 64, 64), 64)
+        acc = jnp.zeros((64, 128), F32)
+        for k in range(D // 128):
+            v = x_v[r, k * 128 : (k + 1) * 128].astype(F32)
+            acc = acc + v * v
+        inv = lax.rsqrt(jnp.sum(acc, axis=-1, keepdims=True) * (1.0 / D) + epsilon)
+        invb[r, :] = jnp.broadcast_to(inv, (64, 128))
+
+    def ag_a():
+        ag2_next((0, 3))
+
+    def ag_b():
+        ag2_next((0, 1))
+
+    def ag_c():
+        ag1_next(1)
+        ag2_first((1, 3))
+        ag2_first((1, 1))
+
+    hidden_steps = {4: ag_a, 12: ag_b, 28: ag_c}
+
     @pl.loop(0, TOK // 16)
     def _(i):
+        for k, fn in hidden_steps.items():
+            pl.when(i == k)(fn)
         r = pl.ds(pl.multiple_of(i * 16, 16), 16)
-        v = x_v[r, :].astype(F32)
-        inv = lax.rsqrt(jnp.mean(v * v, axis=-1, keepdims=True) + epsilon)
-        invb[r, :] = jnp.broadcast_to(inv, (16, 128))
-        hid[r, :] = (x_v[r, :].astype(F32) * inv * grow[0:1, :]).astype(BF)
-
-    def ag_a():
-        ag2_next((0, 0))
-        ag2_first((1, 0))
-
-    def ag_b():
-        ag1_next(1)
-
-    def ag_c():
-        ag2_next((0, 3))
-        ag1_wait(0)
-        ag2_first((0, 2))
+        inv = invb[r, :]
+        for k in range(D // 128):
+            c = slice(k * 128, (k + 1) * 128)
+            v = x_v[r, c].astype(F32) * inv
+            hid[r, c] = (v.reshape(2, 8, 128) * grow[:, c][None]).reshape(16, 128).astype(BF)
 
     def ag_d():
-        ag2_next((0, 1))
-        ag2_first((1, 3))
+        ag2_next((1, 0))
 
     def ag_e():
-        ag2_next((1, 0))
-        ag2_first((1, 1))
-
-    steps = {0: ag_a, 3: ag_b, 6: ag_c, 9: ag_d, 12: ag_e}
+        ag2_next((0, 2))
+        ag1_wait(1)
+        ag2_first((1, 2))
+
+    steps = {4: ag_d, 11: ag_e}
 
     @pl.loop(0, 16)
     def _(i):
@@ -432,47 +454,12 @@
         pt[pl.ds(r0, 1024), :] = res[:, :128].astype(BF)
         pt[pl.ds(r0 + 1024, 1024), :] = res[:, 128:].astype(BF)
 
-    ag1_wait(1)
-    ag2_first((1, 2))
-    ag2_next((0, 2))
-
-    ps_wait(1)
-    ps_sent(1)
-
-    @pl.loop(0, 12)
-    def _(i):
-        r = pl.ds(pl.multiple_of(i * 16, 16), 16)
-        rm = pl.ds(pl.multiple_of(mine + i * 16, 16), 16)
-        ps[rm, :] = psum[r, :] + srecv[r, :]
-
-    ps_send(2)
+    order = SCATTER_ORDER
     ag2_next((1, 3))
     ag2_next((1, 1))
-    ps_wait(2)
-    ps_sent(2)
-    loads["om"].wait()
-    loads["gp"].wait()
-    loads["lp"].wait()
-
-    def update(r, total):
-        average = total * 0.25
-        m = momentum_rate * om[r, :] + average
-        gn = gp[r, :] - outer_rate * (average + momentum_rate * m)
-        mom_out[r, :] = m
-        glob_out[r, :] = gn
-        loc_out[r, :] = (mixing_rate * lp[r, :].astype(F32) + (1.0 - mixing_rate) * gn).astype(BF)
-
-    @pl.loop(0, 12)
-    def _(i):
-        rm = pl.ds(pl.multiple_of(mine + i * 16, 16), 16)
-        update(rm, ps[rm, :])
-        ro = pl.ds(pl.multiple_of(other + i * 16, 16), 16)
-        update(ro, trecv[pl.ds(pl.multiple_of(i * 16, 16), 16), :])
-
-    ag2_next((1, 2))
-    order = SCATTER_ORDER
     rs_first(1, order[0])
     rs_first(1, order[1])
+    ag2_next((1, 2))
     for yr in range(2):
         for o in range(4):
             ag2_wait((yr, o))
@@ -555,6 +542,17 @@
                 kv_out[:, c128] = pre[:, b * 128 : (b + 1) * 128].astype(BF)
 
     cb[...] = jnp.broadcast_to(jnp.sum(cb[...], axis=-1, keepdims=True) * (1.0 / D), (TOK, 128))
+
+    ps_wait(1)
+    ps_sent(1)
+
+    @pl.loop(0, 4)
+    def _(i):
+        r = pl.ds(pl.multiple_of(i * 48, 16), 48)
+        rm = pl.ds(pl.multiple_of(mine + i * 48, 16), 48)
+        ps[rm, :] = psum[r, :].astype(F32) + srecv[r, :].astype(F32)
+
+    ps_send(2)
 
     bwd_steps = {0: r3, 2: r4, 4: r4b, 5: r5, 8: r6, 10: r6b, 12: r7, 15: r8}
 
@@ -574,6 +572,27 @@
             ig_out[:, cols] = (inv * (ng - normed * cb[...])).astype(BF)
 
     r9()
+    ps_wait(2)
+    ps_sent(2)
+    loads["om"].wait()
+    loads["gp"].wait()
+    loads["lp"].wait()
+
+    def update(r, total):
+        average = total * 0.25
+        m = momentum_rate * om[r, :] + average
+        gn = gp[r, :] - outer_rate * (average + momentum_rate * m)
+        mom_out[r, :] = m
+        glob_out[r, :] = gn
+        loc_out[r, :] = (mixing_rate * lp[r, :].astype(F32) + (1.0 - mixing_rate) * gn).astype(BF)
+
+    @pl.loop(0, 12)
+    def _(i):
+        rm = pl.ds(pl.multiple_of(mine + i * 16, 16), 16)
+        update(rm, ps[rm, :])
+        ro = pl.ds(pl.multiple_of(other + i * 16, 16), 16)
+        update(ro, trecv[pl.ds(pl.multiple_of(i * 16, 16), 16), :])
+
     rs_last(2, 0)
     rs_y_wait()
     scale = 1.0 / math.sqrt(TOK * 32)
@@ -656,8 +675,8 @@
             pltpu.VMEM((TOK, 128), F32),
             pltpu.VMEM((PSR, KV), F32),
             pltpu.VMEM((PSR // 2, KV), F32),
-            pltpu.VMEM((PSR // 2, KV), F32),
-            pltpu.VMEM((PSR // 2, KV), F32),
+            pltpu.VMEM((PSR // 2, KV), BF),
+            pltpu.VMEM((PSR // 2, KV), BF),
             pltpu.VMEM((PSR // 2, KV), F32),
             pltpu.VMEM((PSR, KV), F32),
             pltpu.VMEM((PSR, KV), F32),

time: 117 us -> 105 us (0.90)
  Pallas kernels: 116 us -> 104 us
    pallas_call x1, Pallas kernels: 113 us -> 100 us  [local(): pl.pallas_call(kernel, out_shape=(pltpu.VMEM((TOK, KV), BF), pltpu.VMEM((...]
where the time goes in v3:
time: 105 us; the launch traced here: 104 us
  Pallas kernels  104 us (99%)
    pallas_call x1, Pallas kernels, local(): pl.pallas_call(kernel, out_shape=(pltpu.VMEM((TOK, KV), BF), pltpu.VMEM((...  100 us
    pallas_call x1, Pallas kernels, local(): pl.pallas_call(write_kernel, out_shape=tuple((jax.ShapeDtypeStruct(o.shap...  3.78 us

profile of v3, /device:TPU:0, one launch (start us, length us, event | category | flops | bytes accessed | tf_op | source)
XLA Modules:
  0.0 104.4 jit_solution(1268227687050833700)
XLA Ops:
  0.6 100.0 %shard_map.135 = (bf16[512,1024]{1,0:T(8,128)(2,1)S(1)}, bf16[512,4096]{1,0:T(8,128)(2,1)S(1)}, f32[128,1024]{1,0:T(8,128)S(1)}, f32[1,128]{1,0:T(1,128)S(1)}, f...) custom-call(bf16[512,4096]{1,0:T(8,128)(2,1)} %bitcast.9, bf16[1,128]{1,0:T(2,128)(2,1)} %gain_v.1, ...), custom_call_target="tpu_custom_call" | custom-call | tf_op jit(solution)/shard_map/pallas_call | solution.py:646
  100.6 3.8 %shard_map.136 = (bf16[512,1024]{1,0:T(8,128)(2,1)}, bf16[512,4096]{1,0:T(8,128)(2,1)}, f32[128,1024]{1,0:T(8,128)}, f32[1,128]{1,0:T(1,128)}, f32[384,1024]{1,0...) custom-call(bf16[512,1024]{1,0:T(8,128)(2,1)S(1)} %get-tuple-element.21.refs_0_, ...), custom_call_target="tpu_custom_call" | custom-call | tf_op jit(solution)/shard_map/pallas_call | solution.py:707
